TPU v7x, 32 devices: a whole 2x2x4 slice. The times are simulated.
32 devices in a mesh: seq: 4 (over y, x), chan: 8 (over z, core).
Axes of the slice: x: 2, y: 2, z: 4, core: 2. Of those that a mesh axis runs over, the one named last changes fastest.
Arguments:
- hidden: bfloat16 [4096, 1024], P('chan', 'seq'), may hold values from -70 to 70
- gate_in: bfloat16 [4096, 1024], P('chan', 'seq'), may hold values from -4 to 4
- gate_out: bfloat16 [4096, 1024], P('chan', 'seq'), may hold values from -4 to 4
- filters: float32 [4096, 1024], P('chan', 'seq'), may hold values from -0.1875 to 0.1875
- norm_gain: float32 [4096], P('chan'), may hold values from 0.1 to 1.9
- skip_weight: float32 [4096], P('chan'), may hold values from -4 to 4
Outputs:
- mixed: bfloat16 [4096, 1024], P('chan', 'seq')
All inputs are finite; a program needn't handle non-finite values.
Results may differ from a plain program's by a relative error of at most 0.0025.
Values sent between devices are 32-bit elements; how exact they have to be, the bound alone decides.
A program may use at most 64 MiB of HBM per device.

v0:
```python
import functools
import math

import jax
import jax.numpy as jnp
import numpy as np
from jax import lax
from jax.experimental import pallas as pl
from jax.experimental.pallas import tpu as pltpu
from jax.sharding import PartitionSpec as P

highest = lax.Precision.HIGHEST
epsilon = 1e-06


def angle_table(row_count, col_count, period, sign):
    row_index = lax.iota(jnp.int32, row_count)[:, None]
    col_index = lax.iota(jnp.int32, col_count)[None, :]
    phase = (row_index * col_index % period).astype(jnp.float32) * (2.0 * math.pi / period)
    return (jnp.cos(phase), sign * jnp.sin(phase))


def twiddle_table(row_count, col_count, span, offset, period, sign):
    row_index = lax.iota(jnp.int32, row_count)[:, None]
    col_index = (lax.iota(jnp.int32, col_count) % span + offset)[None, :]
    phase = (row_index * col_index % period).astype(jnp.float32) * (2.0 * math.pi / period)
    return (jnp.cos(phase), sign * jnp.sin(phase))


def rotate(left_real, left_imag, right_real, right_imag):
    return (
        left_real * right_real - left_imag * right_imag,
        left_real * right_imag + left_imag * right_real,
    )


def sequence_forward(block, groups, span, offset, period):
    rows = 2 * groups
    cosine, sine = angle_table(rows, groups, rows, -1.0)
    both = jnp.dot(jnp.concatenate([cosine, sine], axis=0), block, precision=highest)
    real_part, imag_part = (both[:rows], both[rows:])
    turn_real, turn_imag = twiddle_table(rows, block.shape[1], span, offset, period, -1.0)
    return rotate(real_part, imag_part, turn_real, turn_imag)


def sequence_inverse(real_part, imag_part, groups, span, offset, period):
    rows = 2 * groups
    turn_real, turn_imag = twiddle_table(rows, real_part.shape[1], span, offset, period, 1.0)
    real_part, imag_part = rotate(real_part, imag_part, turn_real, turn_imag)
    cosine, sine = angle_table(groups, rows, rows, 1.0)
    return jnp.dot(cosine, real_part, precision=highest) - jnp.dot(
        sine, imag_part, precision=highest
    )


def full_transform(stacked, sign):
    length = stacked.shape[1]
    cosine, sine = angle_table(length, length, length, sign)
    return jnp.dot(stacked, jnp.concatenate([cosine, sine], axis=1), precision=highest)


def spectral_product(signal_real, signal_imag, filter_real, filter_imag):
    count, length = signal_real.shape
    stacked = jnp.concatenate([signal_real, signal_imag, filter_real, filter_imag], axis=0)
    spectra = full_transform(stacked, -1.0)
    s_real = spectra[:count, :length] - spectra[count : 2 * count, length:]
    s_imag = spectra[:count, length:] + spectra[count : 2 * count, :length]
    f_real = spectra[2 * count : 3 * count, :length] - spectra[3 * count :, length:]
    f_imag = spectra[2 * count : 3 * count, length:] + spectra[3 * count :, :length]
    product_real, product_imag = rotate(s_real, s_imag, f_real, f_imag)
    back = full_transform(jnp.concatenate([product_real, product_imag], axis=0), 1.0)
    return (
        back[:count, :length] - back[count:, length:],
        back[:count, length:] + back[count:, :length],
    )


def four_step(signal, filters, groups, width, period):
    channels, positions = signal.shape
    spread_signal, spread_filter = (
        lax.all_to_all(signal, "seq", split_axis=1, concat_axis=0, tiled=True),
        lax.all_to_all(filters, "seq", split_axis=1, concat_axis=0, tiled=True),
    )
    flat = (groups, channels * width)
    offset = lax.axis_index("seq") * width
    signal_real, signal_imag = sequence_forward(
        spread_signal.reshape(flat), groups, width, offset, period
    )
    filter_real, filter_imag = sequence_forward(
        spread_filter.reshape(flat), groups, width, offset, period
    )
    middle = (2 * groups, channels, width)
    signal_real, signal_imag, filter_real, filter_imag = (
        lax.all_to_all(signal_real.reshape(middle), "seq", split_axis=0, concat_axis=2, tiled=True),
        lax.all_to_all(signal_imag.reshape(middle), "seq", split_axis=0, concat_axis=2, tiled=True),
        lax.all_to_all(filter_real.reshape(middle), "seq", split_axis=0, concat_axis=2, tiled=True),
        lax.all_to_all(filter_imag.reshape(middle), "seq", split_axis=0, concat_axis=2, tiled=True),
    )
    rows = (2 * channels, positions)
    back_real, back_imag = spectral_product(
        signal_real.reshape(rows),
        signal_imag.reshape(rows),
        filter_real.reshape(rows),
        filter_imag.reshape(rows),
    )
    split = (2, channels, positions)
    back_real, back_imag = (
        lax.all_to_all(back_real.reshape(split), "seq", split_axis=2, concat_axis=0, tiled=True),
        lax.all_to_all(back_imag.reshape(split), "seq", split_axis=2, concat_axis=0, tiled=True),
    )
    wide = (2 * groups, channels * width)
    field = sequence_inverse(
        back_real.reshape(wide), back_imag.reshape(wide), groups, width, offset, period
    )
    result = lax.all_to_all(
        field.reshape(groups, channels, width), "seq", split_axis=0, concat_axis=2, tiled=True
    )
    return result.reshape(channels, positions) / period


def split_table(table):
    high = table.astype(jnp.bfloat16)
    low = (table - high.astype(np.float64)).astype(jnp.bfloat16)
    return high, low


def transform_tables(length, chunk, blocks):
    place = np.arange(length)[:, None]
    odd = 2 * np.arange(length)[None, :] + 1
    phase = (place * odd % (4 * length)) * (2.0 * np.pi / (4 * length))
    chunks = length // chunk
    cosine = np.cos(phase).reshape(length, chunks, chunk)
    sine = np.sin(phase).reshape(length, chunks, chunk)
    both = np.concatenate([cosine, -sine], axis=2)
    forward = both.transpose(1, 0, 2)
    inverse = both.reshape(length, 2 * length).T / length
    inverse = inverse.reshape(2 * length, blocks, length // blocks).transpose(1, 0, 2)
    return split_table(forward) + split_table(inverse)


def halves(value):
    high = value.astype(jnp.bfloat16)
    return high, (value - high.astype(jnp.float32)).astype(jnp.bfloat16)


def column(row, count, width):
    square = jnp.transpose(jnp.broadcast_to(row, (128, count)))
    return jnp.concatenate([square] * (width // 128), axis=1)


def conv_kernel(
    groups, peers, hidden, gate_in, gate_out, filters, gain, skip, fwd_hi, fwd_lo, inv_hi, inv_lo,
    mixed,
    fh, fl, ih, il, filter_in, signal_in, conv_in, conv_out, signal, local_sum, sums, halved, spectrum, product,
    table_sem, own_sem, f_send, f_recv, s_send, s_recv, c_send, c_recv, q_send, q_recv,
):
    me = lax.axis_index("seq")
    row = lax.axis_index("chan")
    count = hidden.shape[0] // groups
    width = hidden.shape[1]

    barrier = pltpu.get_barrier_semaphore()
    for step in range(1, groups):
        pl.semaphore_signal(
            barrier, inc=1, device_id={"seq": lax.rem(me + step, groups)}, device_id_type=pl.DeviceIdType.MESH
        )
    for step in range(1, peers):
        pl.semaphore_signal(
            barrier, inc=1, device_id={"chan": lax.rem(row + step, peers)}, device_id_type=pl.DeviceIdType.MESH
        )
    pl.semaphore_wait(barrier, groups + peers - 2)

    def send(step, source, target, sent, received):
        to = lax.rem(me + step, groups)
        copy = pltpu.make_async_remote_copy(
            src_ref=source.at[to], dst_ref=target.at[me], send_sem=sent.at[step], recv_sem=received.at[step],
            device_id={"seq": to}, device_id_type=pl.DeviceIdType.MESH,
        )
        copy.start()
        return copy

    order = [groups // 2] + [s for s in range(1, groups) if s != groups // 2]
    filter_copies = []
    for step in range(1, groups):
        to = lax.rem(me + step, groups)
        copy = pltpu.make_async_remote_copy(
            src_ref=filters.at[pl.ds(to * count, count), :], dst_ref=filter_in.at[me],
            send_sem=f_send.at[step], recv_sem=f_recv.at[step],
            device_id={"seq": to}, device_id_type=pl.DeviceIdType.MESH,
        )
        copy.start()
        filter_copies.append(copy)
    own_filter = pltpu.make_async_copy(filters.at[pl.ds(me * count, count), :], filter_in.at[me], own_sem.at[0])
    own_filter.start()
    tables = []
    for index, (source, target) in enumerate(((fwd_hi, fh), (fwd_lo, fl), (inv_hi, ih), (inv_lo, il))):
        copy = pltpu.make_async_copy(source, target, table_sem.at[index])
        copy.start()
        tables.append(copy)

    partial = jnp.zeros((1, width), jnp.float32)
    for block in range(groups):
        activity = hidden[block * count : (block + 1) * count, :].astype(jnp.float32)
        partial = partial + jnp.sum(activity * activity, axis=0, keepdims=True)
    local_sum[...] = partial
    sums[row] = partial
    sum_copies = []
    for step in range(1, peers):
        copy = pltpu.make_async_remote_copy(
            src_ref=local_sum, dst_ref=sums.at[row], send_sem=q_send.at[step], recv_sem=q_recv.at[step],
            device_id={"chan": lax.rem(row + step, peers)}, device_id_type=pl.DeviceIdType.MESH,
        )
        copy.start()
        sum_copies.append(copy)
    for copy in sum_copies:
        copy.wait()
    total = sums[0]
    for index in range(1, peers):
        total = total + sums[index]
    scale = lax.rsqrt(total / (hidden.shape[0] * peers) + epsilon)
    for block in range(groups):
        rows = slice(block * count, (block + 1) * count)
        normed = hidden[rows, :].astype(jnp.float32) * scale * column(gain[:, rows], count, width)
        signal[block] = gate_in[rows, :].astype(jnp.float32) * normed
    signal_copies = [send(step, signal, signal_in, s_send, s_recv) for step in range(1, groups)]
    own_signal = pltpu.make_async_copy(signal.at[me], signal_in.at[me], own_sem.at[1])
    own_signal.start()

    def load_halves(source):
        for block in range(groups):
            high, low = halves(source[block])
            halved[:count, block * width : (block + 1) * width] = high
            halved[count:, block * width : (block + 1) * width] = low

    def transform(index):
        both = jnp.dot(halved[...], fh[index], preferred_element_type=jnp.float32)
        small = jnp.dot(halved[:count, :], fl[index], preferred_element_type=jnp.float32)
        return both[:count] + (both[count:] + small)

    chunks = fh.shape[0]
    chunk = fh.shape[2] // 2
    for copy in filter_copies:
        copy.wait()
    own_filter.wait()
    load_halves(filter_in)
    tables[0].wait()
    tables[1].wait()

    def filter_step(index, carry):
        spectrum[index] = transform(index)
        return carry

    lax.fori_loop(0, chunks, filter_step, 0)
    for copy in signal_copies:
        copy.wait()
    own_signal.wait()
    load_halves(signal_in)

    for index in range(chunks):
        s_both = transform(index)
        s_real, s_imag = s_both[:, :chunk], s_both[:, chunk:]
        f_both = spectrum[index]
        f_real, f_imag = f_both[:, :chunk], f_both[:, chunk:]
        real_high, real_low = halves(s_real * f_real - s_imag * f_imag)
        imag_high, imag_low = halves(s_real * f_imag + s_imag * f_real)
        start = 2 * index * chunk
        product[:count, start : start + chunk] = real_high
        product[count:, start : start + chunk] = real_low
        product[:count, start + chunk : start + 2 * chunk] = imag_high
        product[count:, start + chunk : start + 2 * chunk] = imag_low

    tables[2].wait()
    tables[3].wait()

    def invert(block):
        both = jnp.dot(product[...], ih[block], preferred_element_type=jnp.float32)
        small = jnp.dot(product[:count, :], il[block], preferred_element_type=jnp.float32)
        return both[:count] + (both[count:] + small)

    conv_copies = []
    for step in order:
        to = lax.rem(me + step, groups)
        conv_out[to] = invert(to)
        conv_copies.append(send(step, conv_out, conv_in, c_send, c_recv))
    conv_in[me] = invert(me)
    for copy in conv_copies:
        copy.wait()
    for block in range(groups):
        rows = slice(block * count, (block + 1) * count)
        direct = column(skip[:, rows], count, width) * signal[block]
        mixed[rows, :] = (gate_out[rows, :].astype(jnp.float32) * (conv_in[block] + direct)).astype(jnp.bfloat16)


def fused(hidden, gate_in, gate_out, filters, norm_gain, skip_weight):
    channels, width = hidden.shape
    groups, peers = lax.axis_size("seq"), lax.axis_size("chan")
    length, count = groups * width, channels // groups
    chunk = min(256, length)
    tables = [jnp.asarray(t) for t in transform_tables(length, chunk, groups)]
    vmem = pl.BlockSpec(memory_space=pltpu.VMEM)
    hbm = pl.BlockSpec(memory_space=pl.ANY)
    block = (groups, count, width)
    f32, bf16 = jnp.float32, jnp.bfloat16
    pair = pltpu.SemaphoreType.DMA((groups,))
    ring = pltpu.SemaphoreType.DMA((peers,))
    return pl.pallas_call(
        functools.partial(conv_kernel, groups, peers),
        out_shape=jax.ShapeDtypeStruct((channels, width), bf16),
        in_specs=[vmem, vmem, vmem, hbm, vmem, vmem, hbm, hbm, hbm, hbm],
        out_specs=vmem,
        scratch_shapes=[
            pltpu.VMEM(tables[0].shape, bf16),
            pltpu.VMEM(tables[1].shape, bf16),
            pltpu.VMEM(tables[2].shape, bf16),
            pltpu.VMEM(tables[3].shape, bf16),
            pltpu.VMEM(block, f32),
            pltpu.VMEM(block, f32),
            pltpu.VMEM(block, f32),
            pltpu.VMEM(block, f32),
            pltpu.VMEM(block, f32),
            pltpu.VMEM((1, width), f32),
            pltpu.VMEM((peers, 1, width), f32),
            pltpu.VMEM((2 * count, length), bf16),
            pltpu.VMEM((length // chunk, count, 2 * chunk), f32),
            pltpu.VMEM((2 * count, 2 * length), bf16),
            pltpu.SemaphoreType.DMA((4,)),
            pltpu.SemaphoreType.DMA((2,)),
            pair, pair, pair, pair, pair, pair, ring, ring,
        ],
        compiler_params=pltpu.CompilerParams(
            collective_id=0, has_side_effects=True, vmem_limit_bytes=56 * 1024 * 1024
        ),
    )(hidden, gate_in, gate_out, filters, norm_gain.reshape(1, channels), skip_weight.reshape(1, channels), *tables)


def per_device(hidden, gate_in, gate_out, filters, norm_gain, skip_weight):
    length = hidden.shape[1] * lax.axis_size("seq")
    if 16 * length * length <= 2**24 and hidden.shape[0] == 128 * lax.axis_size("seq"):
        return fused(hidden, gate_in, gate_out, filters, norm_gain, skip_weight)
    activity = hidden.astype(jnp.float32)
    channels, positions = activity.shape
    squares = lax.psum(jnp.sum(activity * activity, axis=0), "chan")
    mean_sq = squares / (channels * lax.axis_size("chan")) + epsilon
    normed = activity * lax.rsqrt(mean_sq)[None, :] * norm_gain[:, None]
    signal = gate_in.astype(jnp.float32) * normed
    groups = lax.axis_size("seq")
    width = positions // groups
    period = 2 * positions * groups
    conv = four_step(signal, filters, groups, width, period)
    mixed = gate_out.astype(jnp.float32) * (conv + skip_weight[:, None] * signal)
    return mixed.astype(jnp.bfloat16)


def solution(mesh):
    placed = (
        P("chan", "seq"),
        P("chan", "seq"),
        P("chan", "seq"),
        P("chan", "seq"),
        P("chan"),
        P("chan"),
    )
    return jax.shard_map(
        per_device, mesh=mesh, in_specs=placed, out_specs=P("chan", "seq"), check_vma=False
    )
```

profile of v0, /device:TPU:0, one launch (start us, length us, event | category | flops | bytes accessed | tf_op | source)
XLA Modules:
  0.0 34.5 jit_solution(12297872311209549969)
XLA Ops:
  0.0 32.8 %shard_map.100 = bf16[512,256]{1,0:T(8,128)(2,1)} custom-call(bf16[512,256]{1,0:T(8,128)(2,1)} %hidden.1, bf16[512,256]{1,0:T(8,128)(2,1)} %gate_in.1, bf16[512,256]{1,0:T(8,128)(2,1)} %gate_out.1, f32[512,256]{1,0:T(8,128)} %filters.1, f32[1,512]{1,0:T(1,128)} %bitcast.2, f32[1,512]{1,0:T(1,128)} %bitcast.3, bf16[4,1024,512]{2,1,0:T(8,128)(2,1)} %constant.8.clone.fwd_hi, ...), custom_call_target="tpu_custom_call" | custom-call | tf_op jit(solution)/shard_map/pallas_call | solution.py:306
  32.8 1.7 %copy.12 = bf16[512,256]{1,0:T(8,128)(2,1)} copy(bf16[512,256]{1,0:T(8,128)(2,1)} %shard_map.100) | data formatting | bytes 524288
where the time goes:
time: 34.6 us; the launch traced here: 34.5 us
  Pallas kernels  32.8 us (95%)
  local copies, waits for them, and re-layouts  1.67 us (5%)
    pallas_call x1, Pallas kernels, fused(): pl.pallas_call(functools.partial(conv_kernel, groups, peers), out_shape=j...  32.8 us
    unnamed x1, local copies, waits for them, and re-layouts  1.67 us

commit v1 on v0

--- a/solution.py
+++ b/solution.py
@@ -149,15 +149,32 @@
 
 
 def conv_kernel(
-    groups, peers, hidden, gate_in, gate_out, filters, gain, skip, fwd_hi, fwd_lo, inv_hi, inv_lo,
-    mixed,
-    fh, fl, ih, il, filter_in, signal_in, conv_in, conv_out, signal, local_sum, sums, halved, spectrum, product,
-    table_sem, own_sem, f_send, f_recv, s_send, s_recv, c_send, c_recv, q_send, q_recv,
+    groups, peers, hidden_hbm, gate_hbm, filters, gain, fwd_hi, fwd_lo, inv_hi, inv_lo,
+    conv_in, scale_out,
+    fh, fl, ih, il, hidden, gate_in, filter_in, signal_in, conv_out, signal, local_sum, sums, scales, halved, spectrum,
+    product,
+    table_sem, own_sem, f_send, f_recv, s_send, s_recv, c_send, c_recv, r_send, r_recv, q_send, q_recv,
 ):
     me = lax.axis_index("seq")
     row = lax.axis_index("chan")
     count = hidden.shape[0] // groups
     width = hidden.shape[1]
+
+    def local(source, target, sem):
+        copy = pltpu.make_async_copy(source, target, sem)
+        copy.start()
+        return copy
+
+    def rows_of(block):
+        return pl.ds(pl.multiple_of(block * count, count), count)
+
+    def send(step, source, target, sent, received):
+        copy = pltpu.make_async_remote_copy(
+            src_ref=source, dst_ref=target, send_sem=sent.at[step], recv_sem=received.at[step],
+            device_id={"seq": lax.rem(me + step, groups)}, device_id_type=pl.DeviceIdType.MESH,
+        )
+        copy.start()
+        return copy
 
     barrier = pltpu.get_barrier_semaphore()
     for step in range(1, groups):
@@ -168,42 +185,27 @@
         pl.semaphore_signal(
             barrier, inc=1, device_id={"chan": lax.rem(row + step, peers)}, device_id_type=pl.DeviceIdType.MESH
         )
-    pl.semaphore_wait(barrier, groups + peers - 2)
-
-    def send(step, source, target, sent, received):
-        to = lax.rem(me + step, groups)
-        copy = pltpu.make_async_remote_copy(
-            src_ref=source.at[to], dst_ref=target.at[me], send_sem=sent.at[step], recv_sem=received.at[step],
-            device_id={"seq": to}, device_id_type=pl.DeviceIdType.MESH,
-        )
-        copy.start()
-        return copy
-
-    order = [groups // 2] + [s for s in range(1, groups) if s != groups // 2]
-    filter_copies = []
-    for step in range(1, groups):
-        to = lax.rem(me + step, groups)
-        copy = pltpu.make_async_remote_copy(
-            src_ref=filters.at[pl.ds(to * count, count), :], dst_ref=filter_in.at[me],
-            send_sem=f_send.at[step], recv_sem=f_recv.at[step],
-            device_id={"seq": to}, device_id_type=pl.DeviceIdType.MESH,
-        )
-        copy.start()
-        filter_copies.append(copy)
-    own_filter = pltpu.make_async_copy(filters.at[pl.ds(me * count, count), :], filter_in.at[me], own_sem.at[0])
-    own_filter.start()
-    tables = []
-    for index, (source, target) in enumerate(((fwd_hi, fh), (fwd_lo, fl), (inv_hi, ih), (inv_lo, il))):
-        copy = pltpu.make_async_copy(source, target, table_sem.at[index])
-        copy.start()
-        tables.append(copy)
-
+    own_hidden = local(hidden_hbm, hidden, own_sem.at[1])
+    own_gate = local(gate_hbm, gate_in, own_sem.at[2])
+    own_filter = local(filters.at[rows_of(me), :], filter_in.at[me], own_sem.at[0])
+    tables = [
+        local(source, target, table_sem.at[index])
+        for index, (source, target) in enumerate(((fwd_hi, fh), (fwd_lo, fl), (inv_hi, ih), (inv_lo, il)))
+    ]
+    own_hidden.wait()
     partial = jnp.zeros((1, width), jnp.float32)
     for block in range(groups):
         activity = hidden[block * count : (block + 1) * count, :].astype(jnp.float32)
         partial = partial + jnp.sum(activity * activity, axis=0, keepdims=True)
     local_sum[...] = partial
     sums[row] = partial
+    pl.semaphore_wait(barrier, groups + peers - 2)
+
+    order = [groups // 2] + [s for s in range(1, groups) if s != groups // 2]
+    filter_copies = [
+        send(step, filters.at[rows_of(lax.rem(me + step, groups)), :], filter_in.at[me], f_send, f_recv)
+        for step in range(1, groups)
+    ]
     sum_copies = []
     for step in range(1, peers):
         copy = pltpu.make_async_remote_copy(
@@ -212,25 +214,34 @@
         )
         copy.start()
         sum_copies.append(copy)
+
+    def gated(block):
+        rows = rows_of(block)
+        scaled = hidden[rows, :].astype(jnp.float32) * column(gain[block], count, width)
+        return gate_in[rows, :].astype(jnp.float32) * scaled
+
+    own_gate.wait()
+    signal_copies = []
+    for step in range(1, groups):
+        to = lax.rem(me + step, groups)
+        signal[to] = gated(to)
+        signal_copies.append(send(step, signal.at[to], signal_in.at[me], s_send, s_recv))
+    signal_in[me] = gated(me)
+
     for copy in sum_copies:
         copy.wait()
     total = sums[0]
     for index in range(1, peers):
         total = total + sums[index]
     scale = lax.rsqrt(total / (hidden.shape[0] * peers) + epsilon)
-    for block in range(groups):
-        rows = slice(block * count, (block + 1) * count)
-        normed = hidden[rows, :].astype(jnp.float32) * scale * column(gain[:, rows], count, width)
-        signal[block] = gate_in[rows, :].astype(jnp.float32) * normed
-    signal_copies = [send(step, signal, signal_in, s_send, s_recv) for step in range(1, groups)]
-    own_signal = pltpu.make_async_copy(signal.at[me], signal_in.at[me], own_sem.at[1])
-    own_signal.start()
-
-    def load_halves(source):
-        for block in range(groups):
-            high, low = halves(source[block])
-            halved[:count, block * width : (block + 1) * width] = high
-            halved[count:, block * width : (block + 1) * width] = low
+    scale_out[...] = scale
+    scales[me] = scale
+    scale_copies = [send(step, scales.at[me], scales.at[me], r_send, r_recv) for step in range(1, groups)]
+
+    def store_halves(block, value):
+        high, low = halves(value)
+        halved[:count, block * width : (block + 1) * width] = high
+        halved[count:, block * width : (block + 1) * width] = low
 
     def transform(index):
         both = jnp.dot(halved[...], fh[index], preferred_element_type=jnp.float32)
@@ -242,7 +253,8 @@
     for copy in filter_copies:
         copy.wait()
     own_filter.wait()
-    load_halves(filter_in)
+    for block in range(groups):
+        store_halves(block, filter_in[block])
     tables[0].wait()
     tables[1].wait()
 
@@ -251,10 +263,10 @@
         return carry
 
     lax.fori_loop(0, chunks, filter_step, 0)
-    for copy in signal_copies:
+    for copy in signal_copies + scale_copies:
         copy.wait()
-    own_signal.wait()
-    load_halves(signal_in)
+    for block in range(groups):
+        store_halves(block, signal_in[block] * scales[block])
 
     for index in range(chunks):
         s_both = transform(index)
@@ -281,14 +293,12 @@
     for step in order:
         to = lax.rem(me + step, groups)
         conv_out[to] = invert(to)
-        conv_copies.append(send(step, conv_out, conv_in, c_send, c_recv))
-    conv_in[me] = invert(me)
+        conv_copies.append(send(step, conv_out.at[to], conv_in.at[me], c_send, c_recv))
+    conv_out[me] = invert(me)
+    own_conv = local(conv_out.at[me], conv_in.at[me], own_sem.at[3])
     for copy in conv_copies:
         copy.wait()
-    for block in range(groups):
-        rows = slice(block * count, (block + 1) * count)
-        direct = column(skip[:, rows], count, width) * signal[block]
-        mixed[rows, :] = (gate_out[rows, :].astype(jnp.float32) * (conv_in[block] + direct)).astype(jnp.bfloat16)
+    own_conv.wait()
 
 
 def fused(hidden, gate_in, gate_out, filters, norm_gain, skip_weight):
@@ -303,34 +313,39 @@
     f32, bf16 = jnp.float32, jnp.bfloat16
     pair = pltpu.SemaphoreType.DMA((groups,))
     ring = pltpu.SemaphoreType.DMA((peers,))
-    return pl.pallas_call(
+    conv, scale = pl.pallas_call(
         functools.partial(conv_kernel, groups, peers),
-        out_shape=jax.ShapeDtypeStruct((channels, width), bf16),
-        in_specs=[vmem, vmem, vmem, hbm, vmem, vmem, hbm, hbm, hbm, hbm],
-        out_specs=vmem,
+        out_shape=[jax.ShapeDtypeStruct(block, f32), jax.ShapeDtypeStruct((1, width), f32)],
+        in_specs=[hbm, hbm, hbm, vmem, hbm, hbm, hbm, hbm],
+        out_specs=[hbm, vmem],
         scratch_shapes=[
             pltpu.VMEM(tables[0].shape, bf16),
             pltpu.VMEM(tables[1].shape, bf16),
             pltpu.VMEM(tables[2].shape, bf16),
             pltpu.VMEM(tables[3].shape, bf16),
-            pltpu.VMEM(block, f32),
+            pltpu.VMEM((channels, width), bf16),
+            pltpu.VMEM((channels, width), bf16),
             pltpu.VMEM(block, f32),
             pltpu.VMEM(block, f32),
             pltpu.VMEM(block, f32),
             pltpu.VMEM(block, f32),
             pltpu.VMEM((1, width), f32),
             pltpu.VMEM((peers, 1, width), f32),
+            pltpu.VMEM((groups, 1, width), f32),
             pltpu.VMEM((2 * count, length), bf16),
             pltpu.VMEM((length // chunk, count, 2 * chunk), f32),
             pltpu.VMEM((2 * count, 2 * length), bf16),
             pltpu.SemaphoreType.DMA((4,)),
-            pltpu.SemaphoreType.DMA((2,)),
-            pair, pair, pair, pair, pair, pair, ring, ring,
+            pltpu.SemaphoreType.DMA((4,)),
+            pair, pair, pair, pair, pair, pair, pair, pair, ring, ring,
         ],
         compiler_params=pltpu.CompilerParams(
             collective_id=0, has_side_effects=True, vmem_limit_bytes=56 * 1024 * 1024
         ),
-    )(hidden, gate_in, gate_out, filters, norm_gain.reshape(1, channels), skip_weight.reshape(1, channels), *tables)
+    )(hidden, gate_in, filters, norm_gain.reshape(groups, 1, count), *tables)
+    signal = gate_in.astype(f32) * (hidden.astype(f32) * norm_gain[:, None]) * scale
+    mixed = gate_out.astype(f32) * (conv.reshape(channels, width) + skip_weight[:, None] * signal)
+    return mixed.astype(bf16)
 
 
 def per_device(hidden, gate_in, gate_out, filters, norm_gain, skip_weight):

time: 34.6 us -> 34.7 us (level)
  other arithmetic: 0 us -> 2.03 us
  local copies, waits for them, and re-layouts: 1.67 us -> 0.02 us
  Pallas kernels: 32.8 us -> 32.4 us
    convert_element_type x0 -> x1, other arithmetic: none -> 2.03 us  [fused(): return mixed.astype(bf16)]
    unnamed x1 -> x10, local copies, waits for them, and re-layouts: 1.67 us -> 0.02 us
    pallas_call x1, Pallas kernels: 32.8 us -> 32.4 us  [fused(): pl.pallas_call(functools.partial(conv_kernel, groups, peers), out_shape=[...]
where the time goes in v1:
time: 34.7 us; the launch traced here: 34.5 us
  Pallas kernels  32.4 us (93%)
  other arithmetic  2.03 us (6%)
    pallas_call x1, Pallas kernels, fused(): pl.pallas_call(functools.partial(conv_kernel, groups, peers), out_shape=[...  32.4 us
    convert_element_type x1, other arithmetic, fused(): return mixed.astype(bf16)  2.03 us

profile of v1, /device:TPU:0, one launch (start us, length us, event | category | flops | bytes accessed | tf_op | source)
XLA Modules:
  0.0 34.5 jit_solution(839749223686594704)
XLA Ops:
  0.0 0.0 copy-start
  0.0 0.0 copy-start.1
  0.0 0.0 copy-start.2
  0.0 0.0 copy-start.3
  0.0 0.0 copy-start.4
  0.0 32.4 %shard_map.100 = (f32[4,128,256]{2,1,0:T(8,128)}, f32[1,256]{1,0:T(1,128)}) custom-call(bf16[512,256]{1,0:T(8,128)(2,1)} %hidden_hbm.1, bf16[512,256]{1,0:T(8,128)(2,1)} %gate_hbm.1, f32[512,256]{1,0:T(8,128)} %filters.1, f32[4,1,128]{2,1,0:T(1,128)} %bitcast.8, bf16[4,1024,512]{2,1,0:T(8,128)(2,1)} %constant.8.clone.fwd_hi, ...), custom_call_target="tpu_custom_call" | custom-call | tf_op jit(solution)/shard_map/pallas_call | solution.py:316
  32.4 0.0 copy-done
  32.4 0.0 copy-done.1
  32.4 0.0 copy-done.2
  32.5 0.0 copy-done.3
  32.5 0.0 copy-done.4
  32.5 2.0 %fusion.1 = bf16[512,256]{1,0:T(8,128)(2,1)} fusion(f32[4,128,256]{2,1,0:T(8,128)} %get-tuple-element.7, bf16[512,256]{1,0:T(8,128)(2,1)S(1)} %copy-done, bf16[512,256]{1,0:T(8,128)(2,1)S(1)} %copy-done.1, bf16[512,256]{1,0:T(8,128)(2,1)S(1)} %copy-done.2, f32[256]{0:T(256)} %bitcast.9, f32[512]{0:T(512)S(1)} %copy-done.3, f32[512]{0:T(512)S(1)} %copy-done.4), kind=kLoop, calls=%fused_computation.2 | loop fusion | flops 1310720 | bytes 1577984 | tf_op jit(solution)/shard_map/convert_element_type | solution.py:348
Async XLA Ops:
  0.0 32.4 %copy-start = (bf16[512,256]{1,0:T(8,128)(2,1)S(1)}, bf16[512,256]{1,0:T(8,128)(2,1)}, u32[]{:S(2)}) copy-start(bf16[512,256]{1,0:T(8,128)(2,1)} %hidden_hbm.1) | copy-start | bytes 786436
  0.0 32.4 %copy-start.1 = (bf16[512,256]{1,0:T(8,128)(2,1)S(1)}, bf16[512,256]{1,0:T(8,128)(2,1)}, u32[]{:S(2)}) copy-start(bf16[512,256]{1,0:T(8,128)(2,1)} %gate_hbm.1) | copy-start | bytes 786436
  0.0 32.4 %copy-start.2 = (bf16[512,256]{1,0:T(8,128)(2,1)S(1)}, bf16[512,256]{1,0:T(8,128)(2,1)}, u32[]{:S(2)}) copy-start(bf16[512,256]{1,0:T(8,128)(2,1)} %param.12) | copy-start | bytes 786436
  0.0 32.5 %copy-start.3 = (f32[512]{0:T(512)S(1)}, f32[512]{0:T(512)}, u32[]{:S(2)}) copy-start(f32[512]{0:T(512)} %param.14) | copy-start | bytes 6148
  0.0 32.5 %copy-start.4 = (f32[512]{0:T(512)S(1)}, f32[512]{0:T(512)}, u32[]{:S(2)}) copy-start(f32[512]{0:T(512)} %param.15) | copy-start | bytes 6148

commit v2 on v1

--- a/solution.py
+++ b/solution.py
@@ -159,18 +159,17 @@
     row = lax.axis_index("chan")
     count = hidden.shape[0] // groups
     width = hidden.shape[1]
+    parts = filter_in.shape[0]
+    sub = count // parts
 
     def local(source, target, sem):
         copy = pltpu.make_async_copy(source, target, sem)
         copy.start()
         return copy
 
-    def rows_of(block):
-        return pl.ds(pl.multiple_of(block * count, count), count)
-
-    def send(step, source, target, sent, received):
+    def send(slot, step, source, target, sent, received):
         copy = pltpu.make_async_remote_copy(
-            src_ref=source, dst_ref=target, send_sem=sent.at[step], recv_sem=received.at[step],
+            src_ref=source, dst_ref=target, send_sem=sent.at[slot], recv_sem=received.at[slot],
             device_id={"seq": lax.rem(me + step, groups)}, device_id_type=pl.DeviceIdType.MESH,
         )
         copy.start()
@@ -187,7 +186,14 @@
         )
     own_hidden = local(hidden_hbm, hidden, own_sem.at[1])
     own_gate = local(gate_hbm, gate_in, own_sem.at[2])
-    own_filter = local(filters.at[rows_of(me), :], filter_in.at[me], own_sem.at[0])
+    own_filters = [
+        local(
+            filters.at[pl.ds(pl.multiple_of(me * count + part * sub, sub), sub), :],
+            filter_in.at[part, me],
+            own_sem.at[3 + parts + part],
+        )
+        for part in range(parts)
+    ]
     tables = [
         local(source, target, table_sem.at[index])
         for index, (source, target) in enumerate(((fwd_hi, fh), (fwd_lo, fl), (inv_hi, ih), (inv_lo, il)))
@@ -202,10 +208,37 @@
     pl.semaphore_wait(barrier, groups + peers - 2)
 
     order = [groups // 2] + [s for s in range(1, groups) if s != groups // 2]
-    filter_copies = [
-        send(step, filters.at[rows_of(lax.rem(me + step, groups)), :], filter_in.at[me], f_send, f_recv)
-        for step in range(1, groups)
-    ]
+
+    def send_filters(part):
+        return [
+            send(
+                part * groups + step,
+                step,
+                filters.at[pl.ds(pl.multiple_of(lax.rem(me + step, groups) * count + part * sub, sub), sub), :],
+                filter_in.at[part, me],
+                f_send,
+                f_recv,
+            )
+            for step in range(1, groups)
+        ]
+
+    def gated(block, part):
+        rows = pl.ds(pl.multiple_of(block * count + part * sub, sub), sub)
+        gains = column(gain[block], count, width)[part * sub : (part + 1) * sub]
+        return gate_in[rows, :].astype(jnp.float32) * (hidden[rows, :].astype(jnp.float32) * gains)
+
+    def send_signal(part):
+        copies = []
+        for step in range(1, groups):
+            to = lax.rem(me + step, groups)
+            signal[part, to] = gated(to, part)
+            copies.append(
+                send(part * groups + step, step, signal.at[part, to], signal_in.at[part, me], s_send, s_recv)
+            )
+        signal_in[part, me] = gated(me, part)
+        return copies
+
+    filter_copies = [send_filters(0)]
     sum_copies = []
     for step in range(1, peers):
         copy = pltpu.make_async_remote_copy(
@@ -214,20 +247,10 @@
         )
         copy.start()
         sum_copies.append(copy)
-
-    def gated(block):
-        rows = rows_of(block)
-        scaled = hidden[rows, :].astype(jnp.float32) * column(gain[block], count, width)
-        return gate_in[rows, :].astype(jnp.float32) * scaled
-
     own_gate.wait()
-    signal_copies = []
-    for step in range(1, groups):
-        to = lax.rem(me + step, groups)
-        signal[to] = gated(to)
-        signal_copies.append(send(step, signal.at[to], signal_in.at[me], s_send, s_recv))
-    signal_in[me] = gated(me)
-
+    signal_copies = [send_signal(0)]
+    for part in range(1, parts):
+        filter_copies.append(send_filters(part))
     for copy in sum_copies:
         copy.wait()
     total = sums[0]
@@ -236,69 +259,76 @@
     scale = lax.rsqrt(total / (hidden.shape[0] * peers) + epsilon)
     scale_out[...] = scale
     scales[me] = scale
-    scale_copies = [send(step, scales.at[me], scales.at[me], r_send, r_recv) for step in range(1, groups)]
+    scale_copies = [send(step, step, scales.at[me], scales.at[me], r_send, r_recv) for step in range(1, groups)]
+    for part in range(1, parts):
+        signal_copies.append(send_signal(part))
+
+    chunks = fh.shape[0]
+    chunk = fh.shape[2] // 2
 
     def store_halves(block, value):
         high, low = halves(value)
-        halved[:count, block * width : (block + 1) * width] = high
-        halved[count:, block * width : (block + 1) * width] = low
+        halved[:sub, block * width : (block + 1) * width] = high
+        halved[sub:, block * width : (block + 1) * width] = low
 
     def transform(index):
         both = jnp.dot(halved[...], fh[index], preferred_element_type=jnp.float32)
-        small = jnp.dot(halved[:count, :], fl[index], preferred_element_type=jnp.float32)
-        return both[:count] + (both[count:] + small)
-
-    chunks = fh.shape[0]
-    chunk = fh.shape[2] // 2
-    for copy in filter_copies:
-        copy.wait()
-    own_filter.wait()
-    for block in range(groups):
-        store_halves(block, filter_in[block])
-    tables[0].wait()
-    tables[1].wait()
+        small = jnp.dot(halved[:sub, :], fl[index], preferred_element_type=jnp.float32)
+        return both[:sub] + (both[sub:] + small)
 
     def filter_step(index, carry):
         spectrum[index] = transform(index)
         return carry
 
-    lax.fori_loop(0, chunks, filter_step, 0)
-    for copy in signal_copies + scale_copies:
-        copy.wait()
-    for block in range(groups):
-        store_halves(block, signal_in[block] * scales[block])
-
-    for index in range(chunks):
-        s_both = transform(index)
-        s_real, s_imag = s_both[:, :chunk], s_both[:, chunk:]
-        f_both = spectrum[index]
-        f_real, f_imag = f_both[:, :chunk], f_both[:, chunk:]
-        real_high, real_low = halves(s_real * f_real - s_imag * f_imag)
-        imag_high, imag_low = halves(s_real * f_imag + s_imag * f_real)
-        start = 2 * index * chunk
-        product[:count, start : start + chunk] = real_high
-        product[count:, start : start + chunk] = real_low
-        product[:count, start + chunk : start + 2 * chunk] = imag_high
-        product[count:, start + chunk : start + 2 * chunk] = imag_low
-
-    tables[2].wait()
-    tables[3].wait()
-
     def invert(block):
         both = jnp.dot(product[...], ih[block], preferred_element_type=jnp.float32)
-        small = jnp.dot(product[:count, :], il[block], preferred_element_type=jnp.float32)
-        return both[:count] + (both[count:] + small)
-
+        small = jnp.dot(product[:sub, :], il[block], preferred_element_type=jnp.float32)
+        return both[:sub] + (both[sub:] + small)
+
+    for copy in own_filters:
+        copy.wait()
     conv_copies = []
-    for step in order:
-        to = lax.rem(me + step, groups)
-        conv_out[to] = invert(to)
-        conv_copies.append(send(step, conv_out.at[to], conv_in.at[me], c_send, c_recv))
-    conv_out[me] = invert(me)
-    own_conv = local(conv_out.at[me], conv_in.at[me], own_sem.at[3])
+    for part in range(parts):
+        for copy in filter_copies[part]:
+            copy.wait()
+        for block in range(groups):
+            store_halves(block, filter_in[part, block])
+        if part == 0:
+            tables[0].wait()
+            tables[1].wait()
+        lax.fori_loop(0, chunks, filter_step, 0)
+        for copy in signal_copies[part]:
+            copy.wait()
+        if part == 0:
+            for copy in scale_copies:
+                copy.wait()
+        for block in range(groups):
+            store_halves(block, signal_in[part, block] * scales[block])
+        for index in range(chunks):
+            s_both = transform(index)
+            s_real, s_imag = s_both[:, :chunk], s_both[:, chunk:]
+            f_both = spectrum[index]
+            f_real, f_imag = f_both[:, :chunk], f_both[:, chunk:]
+            real_high, real_low = halves(s_real * f_real - s_imag * f_imag)
+            imag_high, imag_low = halves(s_real * f_imag + s_imag * f_real)
+            start = 2 * index * chunk
+            product[:sub, start : start + chunk] = real_high
+            product[sub:, start : start + chunk] = real_low
+            product[:sub, start + chunk : start + 2 * chunk] = imag_high
+            product[sub:, start + chunk : start + 2 * chunk] = imag_low
+        if part == 0:
+            tables[2].wait()
+            tables[3].wait()
+        for step in order:
+            to = lax.rem(me + step, groups)
+            conv_out[part, to] = invert(to)
+            conv_copies.append(
+                send(part * groups + step, step, conv_out.at[part, to], conv_in.at[me, part], c_send, c_recv)
+            )
+        conv_out[part, me] = invert(me)
+        conv_copies.append(local(conv_out.at[part, me], conv_in.at[me, part], own_sem.at[3 + part]))
     for copy in conv_copies:
         copy.wait()
-    own_conv.wait()
 
 
 def fused(hidden, gate_in, gate_out, filters, norm_gain, skip_weight):
@@ -309,13 +339,15 @@
     tables = [jnp.asarray(t) for t in transform_tables(length, chunk, groups)]
     vmem = pl.BlockSpec(memory_space=pltpu.VMEM)
     hbm = pl.BlockSpec(memory_space=pl.ANY)
-    block = (groups, count, width)
+    parts = 2
+    sub = count // parts
+    block = (parts, groups, sub, width)
     f32, bf16 = jnp.float32, jnp.bfloat16
-    pair = pltpu.SemaphoreType.DMA((groups,))
+    pair = pltpu.SemaphoreType.DMA((parts * groups,))
     ring = pltpu.SemaphoreType.DMA((peers,))
     conv, scale = pl.pallas_call(
         functools.partial(conv_kernel, groups, peers),
-        out_shape=[jax.ShapeDtypeStruct(block, f32), jax.ShapeDtypeStruct((1, width), f32)],
+        out_shape=[jax.ShapeDtypeStruct((groups, parts, sub, width), f32), jax.ShapeDtypeStruct((1, width), f32)],
         in_specs=[hbm, hbm, hbm, vmem, hbm, hbm, hbm, hbm],
         out_specs=[hbm, vmem],
         scratch_shapes=[
@@ -332,11 +364,11 @@
             pltpu.VMEM((1, width), f32),
             pltpu.VMEM((peers, 1, width), f32),
             pltpu.VMEM((groups, 1, width), f32),
-            pltpu.VMEM((2 * count, length), bf16),
-            pltpu.VMEM((length // chunk, count, 2 * chunk), f32),
-            pltpu.VMEM((2 * count, 2 * length), bf16),
+            pltpu.VMEM((2 * sub, length), bf16),
+            pltpu.VMEM((length // chunk, sub, 2 * chunk), f32),
+            pltpu.VMEM((2 * sub, 2 * length), bf16),
             pltpu.SemaphoreType.DMA((4,)),
-            pltpu.SemaphoreType.DMA((4,)),
+            pltpu.SemaphoreType.DMA((3 + 2 * parts,)),
             pair, pair, pair, pair, pair, pair, pair, pair, ring, ring,
         ],
         compiler_params=pltpu.CompilerParams(

time: 34.7 us -> 34.6 us (level)
  no operation moved by 1% of the time
where the time goes in v2:
time: 34.6 us; the launch traced here: 34.5 us
  Pallas kernels  32.4 us (94%)
  other arithmetic  2.03 us (6%)
    pallas_call x1, Pallas kernels, fused(): pl.pallas_call(functools.partial(conv_kernel, groups, peers), out_shape=[...  32.4 us
    convert_element_type x1, other arithmetic, fused(): return mixed.astype(bf16)  2.03 us

profile of v2, /device:TPU:0, one launch (start us, length us, event | category | flops | bytes accessed | tf_op | source)
XLA Modules:
  0.0 34.5 jit_solution(16015530873296836291)
XLA Ops:
  0.0 0.0 copy-start
  0.0 0.0 copy-start.1
  0.0 0.0 copy-start.2
  0.0 0.0 copy-start.3
  0.0 0.0 copy-start.4
  0.0 32.4 %shard_map.100 = (f32[4,2,64,256]{3,2,1,0:T(8,128)}, f32[1,256]{1,0:T(1,128)}) custom-call(bf16[512,256]{1,0:T(8,128)(2,1)} %hidden_hbm.1, bf16[512,256]{1,0:T(8,128)(2,1)} %gate_hbm.1, f32[512,256]{1,0:T(8,128)} %filters.1, f32[4,1,128]{2,1,0:T(1,128)} %bitcast.8, bf16[4,1024,512]{2,1,0:T(8,128)(2,1)} %constant.8.clone.fwd_hi, ...), custom_call_target="tpu_custom_call" | custom-call | tf_op jit(solution)/shard_map/pallas_call | solution.py:348
  32.4 0.0 copy-done
  32.4 0.0 copy-done.1
  32.4 0.0 copy-done.2
  32.4 0.0 copy-done.3
  32.4 0.0 copy-done.4
  32.4 2.0 %fusion.1 = bf16[512,256]{1,0:T(8,128)(2,1)} fusion(f32[4,2,64,256]{3,2,1,0:T(8,128)} %get-tuple-element.7, bf16[512,256]{1,0:T(8,128)(2,1)S(1)} %copy-done, bf16[512,256]{1,0:T(8,128)(2,1)S(1)} %copy-done.1, bf16[512,256]{1,0:T(8,128)(2,1)S(1)} %copy-done.2, f32[256]{0:T(256)} %bitcast.9, f32[512]{0:T(512)S(1)} %copy-done.3, f32[512]{0:T(512)S(1)} %copy-done.4), kind=kLoop, calls=%fused_computation.2 | loop fusion | flops 1310720 | bytes 1577984 | tf_op jit(solution)/shard_map/convert_element_type | solution.py:380
Async XLA Ops:
  0.0 32.4 %copy-start = (bf16[512,256]{1,0:T(8,128)(2,1)S(1)}, bf16[512,256]{1,0:T(8,128)(2,1)}, u32[]{:S(2)}) copy-start(bf16[512,256]{1,0:T(8,128)(2,1)} %hidden_hbm.1) | copy-start | bytes 786436
  0.0 32.4 %copy-start.1 = (bf16[512,256]{1,0:T(8,128)(2,1)S(1)}, bf16[512,256]{1,0:T(8,128)(2,1)}, u32[]{:S(2)}) copy-start(bf16[512,256]{1,0:T(8,128)(2,1)} %gate_hbm.1) | copy-start | bytes 786436
  0.0 32.4 %copy-start.2 = (bf16[512,256]{1,0:T(8,128)(2,1)S(1)}, bf16[512,256]{1,0:T(8,128)(2,1)}, u32[]{:S(2)}) copy-start(bf16[512,256]{1,0:T(8,128)(2,1)} %param.12) | copy-start | bytes 786436
  0.0 32.4 %copy-start.3 = (f32[512]{0:T(512)S(1)}, f32[512]{0:T(512)}, u32[]{:S(2)}) copy-start(f32[512]{0:T(512)} %param.14) | copy-start | bytes 6148
  0.0 32.4 %copy-start.4 = (f32[512]{0:T(512)S(1)}, f32[512]{0:T(512)}, u32[]{:S(2)}) copy-start(f32[512]{0:T(512)} %param.15) | copy-start | bytes 6148

commit v3 on v2

--- a/solution.py
+++ b/solution.py
@@ -151,15 +151,15 @@
 def conv_kernel(
     groups, peers, hidden_hbm, gate_hbm, filters, gain, fwd_hi, fwd_lo, inv_hi, inv_lo,
     conv_in, scale_out,
-    fh, fl, ih, il, hidden, gate_in, filter_in, signal_in, conv_out, signal, local_sum, sums, scales, halved, spectrum,
+    fh, fl, ih, il, hidden, gate_in, filter_in, signal_in, conv_out, signal, local_sum, sums, halved_filter, halved, spectrum,
     product,
-    table_sem, own_sem, f_send, f_recv, s_send, s_recv, c_send, c_recv, r_send, r_recv, q_send, q_recv,
+    table_sem, own_sem, f_send, f_recv, s_send, s_recv, c_send, c_recv, q_send, q_recv,
 ):
     me = lax.axis_index("seq")
     row = lax.axis_index("chan")
     count = hidden.shape[0] // groups
     width = hidden.shape[1]
-    parts = filter_in.shape[0]
+    parts = signal_in.shape[0]
     sub = count // parts
 
     def local(source, target, sem):
@@ -186,14 +186,9 @@
         )
     own_hidden = local(hidden_hbm, hidden, own_sem.at[1])
     own_gate = local(gate_hbm, gate_in, own_sem.at[2])
-    own_filters = [
-        local(
-            filters.at[pl.ds(pl.multiple_of(me * count + part * sub, sub), sub), :],
-            filter_in.at[part, me],
-            own_sem.at[3 + parts + part],
-        )
-        for part in range(parts)
-    ]
+    own_filter = local(
+        filters.at[pl.ds(pl.multiple_of(me * count, count), count), :], filter_in.at[me], own_sem.at[0]
+    )
     tables = [
         local(source, target, table_sem.at[index])
         for index, (source, target) in enumerate(((fwd_hi, fh), (fwd_lo, fl), (inv_hi, ih), (inv_lo, il)))
@@ -209,36 +204,17 @@
 
     order = [groups // 2] + [s for s in range(1, groups) if s != groups // 2]
 
-    def send_filters(part):
-        return [
-            send(
-                part * groups + step,
-                step,
-                filters.at[pl.ds(pl.multiple_of(lax.rem(me + step, groups) * count + part * sub, sub), sub), :],
-                filter_in.at[part, me],
-                f_send,
-                f_recv,
-            )
-            for step in range(1, groups)
-        ]
-
-    def gated(block, part):
-        rows = pl.ds(pl.multiple_of(block * count + part * sub, sub), sub)
-        gains = column(gain[block], count, width)[part * sub : (part + 1) * sub]
-        return gate_in[rows, :].astype(jnp.float32) * (hidden[rows, :].astype(jnp.float32) * gains)
-
-    def send_signal(part):
-        copies = []
-        for step in range(1, groups):
-            to = lax.rem(me + step, groups)
-            signal[part, to] = gated(to, part)
-            copies.append(
-                send(part * groups + step, step, signal.at[part, to], signal_in.at[part, me], s_send, s_recv)
-            )
-        signal_in[part, me] = gated(me, part)
-        return copies
-
-    filter_copies = [send_filters(0)]
+    filter_copies = [
+        send(
+            step,
+            step,
+            filters.at[pl.ds(pl.multiple_of(lax.rem(me + step, groups) * count, count), count), :],
+            filter_in.at[me],
+            f_send,
+            f_recv,
+        )
+        for step in range(1, groups)
+    ]
     sum_copies = []
     for step in range(1, peers):
         copy = pltpu.make_async_remote_copy(
@@ -248,36 +224,48 @@
         copy.start()
         sum_copies.append(copy)
     own_gate.wait()
-    signal_copies = [send_signal(0)]
-    for part in range(1, parts):
-        filter_copies.append(send_filters(part))
+    for block in range(groups):
+        gains = column(gain[block], count, width)
+        for part in range(parts):
+            rows = slice(block * count + part * sub, block * count + (part + 1) * sub)
+            scaled = hidden[rows, :].astype(jnp.float32) * gains[part * sub : (part + 1) * sub]
+            signal[part, block] = gate_in[rows, :].astype(jnp.float32) * scaled
     for copy in sum_copies:
         copy.wait()
     total = sums[0]
     for index in range(1, peers):
         total = total + sums[index]
     scale = lax.rsqrt(total / (hidden.shape[0] * peers) + epsilon)
+    signal_copies = []
+    for part in range(parts):
+        copies = []
+        for step in range(1, groups):
+            to = lax.rem(me + step, groups)
+            signal[part, to] = signal[part, to] * scale
+            copies.append(
+                send(part * groups + step, step, signal.at[part, to], signal_in.at[part, me], s_send, s_recv)
+            )
+        signal_in[part, me] = signal[part, me] * scale
+        signal_copies.append(copies)
     scale_out[...] = scale
-    scales[me] = scale
-    scale_copies = [send(step, step, scales.at[me], scales.at[me], r_send, r_recv) for step in range(1, groups)]
-    for part in range(1, parts):
-        signal_copies.append(send_signal(part))
 
     chunks = fh.shape[0]
     chunk = fh.shape[2] // 2
 
-    def store_halves(block, value):
+    def store_halves(target, block, value):
+        size = value.shape[0]
         high, low = halves(value)
-        halved[:sub, block * width : (block + 1) * width] = high
-        halved[sub:, block * width : (block + 1) * width] = low
-
-    def transform(index):
-        both = jnp.dot(halved[...], fh[index], preferred_element_type=jnp.float32)
-        small = jnp.dot(halved[:sub, :], fl[index], preferred_element_type=jnp.float32)
-        return both[:sub] + (both[sub:] + small)
+        target[:size, block * width : (block + 1) * width] = high
+        target[size:, block * width : (block + 1) * width] = low
+
+    def transform(source, index):
+        size = source.shape[0] // 2
+        both = jnp.dot(source[...], fh[index], preferred_element_type=jnp.float32)
+        small = jnp.dot(source[:size, :], fl[index], preferred_element_type=jnp.float32)
+        return both[:size] + (both[size:] + small)
 
     def filter_step(index, carry):
-        spectrum[index] = transform(index)
+        spectrum[index] = transform(halved_filter, index)
         return carry
 
     def invert(block):
@@ -285,29 +273,24 @@
         small = jnp.dot(product[:sub, :], il[block], preferred_element_type=jnp.float32)
         return both[:sub] + (both[sub:] + small)
 
-    for copy in own_filters:
+    own_filter.wait()
+    for copy in filter_copies:
         copy.wait()
+    for block in range(groups):
+        store_halves(halved_filter, block, filter_in[block])
+    tables[0].wait()
+    tables[1].wait()
+    lax.fori_loop(0, chunks, filter_step, 0)
     conv_copies = []
     for part in range(parts):
-        for copy in filter_copies[part]:
+        for copy in signal_copies[part]:
             copy.wait()
         for block in range(groups):
-            store_halves(block, filter_in[part, block])
-        if part == 0:
-            tables[0].wait()
-            tables[1].wait()
-        lax.fori_loop(0, chunks, filter_step, 0)
-        for copy in signal_copies[part]:
-            copy.wait()
-        if part == 0:
-            for copy in scale_copies:
-                copy.wait()
-        for block in range(groups):
-            store_halves(block, signal_in[part, block] * scales[block])
+            store_halves(halved, block, signal_in[part, block])
         for index in range(chunks):
-            s_both = transform(index)
+            s_both = transform(halved, index)
             s_real, s_imag = s_both[:, :chunk], s_both[:, chunk:]
-            f_both = spectrum[index]
+            f_both = spectrum[index][part * sub : (part + 1) * sub]
             f_real, f_imag = f_both[:, :chunk], f_both[:, chunk:]
             real_high, real_low = halves(s_real * f_real - s_imag * f_imag)
             imag_high, imag_low = halves(s_real * f_imag + s_imag * f_real)
@@ -357,19 +340,19 @@
             pltpu.VMEM(tables[3].shape, bf16),
             pltpu.VMEM((channels, width), bf16),
             pltpu.VMEM((channels, width), bf16),
-            pltpu.VMEM(block, f32),
+            pltpu.VMEM((groups, count, width), f32),
             pltpu.VMEM(block, f32),
             pltpu.VMEM(block, f32),
             pltpu.VMEM(block, f32),
             pltpu.VMEM((1, width), f32),
             pltpu.VMEM((peers, 1, width), f32),
-            pltpu.VMEM((groups, 1, width), f32),
+            pltpu.VMEM((2 * count, length), bf16),
             pltpu.VMEM((2 * sub, length), bf16),
-            pltpu.VMEM((length // chunk, sub, 2 * chunk), f32),
+            pltpu.VMEM((length // chunk, count, 2 * chunk), f32),
             pltpu.VMEM((2 * sub, 2 * length), bf16),
             pltpu.SemaphoreType.DMA((4,)),
-            pltpu.SemaphoreType.DMA((3 + 2 * parts,)),
-            pair, pair, pair, pair, pair, pair, pair, pair, ring, ring,
+            pltpu.SemaphoreType.DMA((3 + parts,)),
+            pair, pair, pair, pair, pair, pair, ring, ring,
         ],
         compiler_params=pltpu.CompilerParams(
             collective_id=0, has_side_effects=True, vmem_limit_bytes=56 * 1024 * 1024

time: 34.6 us -> 32.5 us (0.939)
  Pallas kernels: 32.4 us -> 30.2 us
    pallas_call x1, Pallas kernels: 32.4 us -> 30.2 us  [fused(): pl.pallas_call(functools.partial(conv_kernel, groups, peers), out_shape=[...]
where the time goes in v3:
time: 32.5 us; the launch traced here: 32.3 us
  Pallas kernels  30.2 us (93%)
  other arithmetic  2.03 us (6%)
    pallas_call x1, Pallas kernels, fused(): pl.pallas_call(functools.partial(conv_kernel, groups, peers), out_shape=[...  30.2 us
    convert_element_type x1, other arithmetic, fused(): return mixed.astype(bf16)  2.03 us

profile of v3, /device:TPU:0, one launch (start us, length us, event | category | flops | bytes accessed | tf_op | source)
XLA Modules:
  0.0 32.3 jit_solution(10202507392876889192)
XLA Ops:
  0.0 0.0 copy-start
  0.0 0.0 copy-start.1
  0.0 0.0 copy-start.2
  0.0 0.0 copy-start.3
  0.0 0.0 copy-start.4
  0.0 30.2 %shard_map.100 = (f32[4,2,64,256]{3,2,1,0:T(8,128)}, f32[1,256]{1,0:T(1,128)}) custom-call(bf16[512,256]{1,0:T(8,128)(2,1)} %hidden_hbm.1, bf16[512,256]{1,0:T(8,128)(2,1)} %gate_hbm.1, f32[512,256]{1,0:T(8,128)} %filters.1, f32[4,1,128]{2,1,0:T(1,128)} %bitcast.8, bf16[4,1024,512]{2,1,0:T(8,128)(2,1)} %constant.8.clone.fwd_hi, ...), custom_call_target="tpu_custom_call" | custom-call | tf_op jit(solution)/shard_map/pallas_call | solution.py:331
  30.2 0.0 copy-done
  30.2 0.0 copy-done.1
  30.3 0.0 copy-done.2
  30.3 0.0 copy-done.3
  30.3 0.0 copy-done.4
  30.3 2.0 %fusion.1 = bf16[512,256]{1,0:T(8,128)(2,1)} fusion(f32[4,2,64,256]{3,2,1,0:T(8,128)} %get-tuple-element.7, bf16[512,256]{1,0:T(8,128)(2,1)S(1)} %copy-done, bf16[512,256]{1,0:T(8,128)(2,1)S(1)} %copy-done.1, bf16[512,256]{1,0:T(8,128)(2,1)S(1)} %copy-done.2, f32[256]{0:T(256)} %bitcast.9, f32[512]{0:T(512)S(1)} %copy-done.3, f32[512]{0:T(512)S(1)} %copy-done.4), kind=kLoop, calls=%fused_computation.2 | loop fusion | flops 1310720 | bytes 1577984 | tf_op jit(solution)/shard_map/convert_element_type | solution.py:363
Async XLA Ops:
  0.0 30.2 %copy-start = (bf16[512,256]{1,0:T(8,128)(2,1)S(1)}, bf16[512,256]{1,0:T(8,128)(2,1)}, u32[]{:S(2)}) copy-start(bf16[512,256]{1,0:T(8,128)(2,1)} %hidden_hbm.1) | copy-start | bytes 786436
  0.0 30.2 %copy-start.1 = (bf16[512,256]{1,0:T(8,128)(2,1)S(1)}, bf16[512,256]{1,0:T(8,128)(2,1)}, u32[]{:S(2)}) copy-start(bf16[512,256]{1,0:T(8,128)(2,1)} %gate_hbm.1) | copy-start | bytes 786436
  0.0 30.3 %copy-start.2 = (bf16[512,256]{1,0:T(8,128)(2,1)S(1)}, bf16[512,256]{1,0:T(8,128)(2,1)}, u32[]{:S(2)}) copy-start(bf16[512,256]{1,0:T(8,128)(2,1)} %param.12) | copy-start | bytes 786436
  0.0 30.3 %copy-start.3 = (f32[512]{0:T(512)S(1)}, f32[512]{0:T(512)}, u32[]{:S(2)}) copy-start(f32[512]{0:T(512)} %param.14) | copy-start | bytes 6148
  0.0 30.3 %copy-start.4 = (f32[512]{0:T(512)S(1)}, f32[512]{0:T(512)}, u32[]{:S(2)}) copy-start(f32[512]{0:T(512)} %param.15) | copy-start | bytes 6148

commit v4 on v3

--- a/solution.py
+++ b/solution.py
@@ -149,8 +149,8 @@
 
 
 def conv_kernel(
-    groups, peers, hidden_hbm, gate_hbm, filters, gain, fwd_hi, fwd_lo, inv_hi, inv_lo,
-    conv_in, scale_out,
+    groups, peers, hidden_hbm, gate_hbm, filters, gain, skip, fwd_hi, fwd_lo, inv_hi, inv_lo,
+    conv_in,
     fh, fl, ih, il, hidden, gate_in, filter_in, signal_in, conv_out, signal, local_sum, sums, halved_filter, halved, spectrum,
     product,
     table_sem, own_sem, f_send, f_recv, s_send, s_recv, c_send, c_recv, q_send, q_recv,
@@ -176,13 +176,13 @@
         return copy
 
     barrier = pltpu.get_barrier_semaphore()
+    for step in range(1, peers):
+        pl.semaphore_signal(
+            barrier, inc=1, device_id={"chan": lax.rem(row + step, peers)}, device_id_type=pl.DeviceIdType.MESH
+        )
     for step in range(1, groups):
         pl.semaphore_signal(
             barrier, inc=1, device_id={"seq": lax.rem(me + step, groups)}, device_id_type=pl.DeviceIdType.MESH
-        )
-    for step in range(1, peers):
-        pl.semaphore_signal(
-            barrier, inc=1, device_id={"chan": lax.rem(row + step, peers)}, device_id_type=pl.DeviceIdType.MESH
         )
     own_hidden = local(hidden_hbm, hidden, own_sem.at[1])
     own_gate = local(gate_hbm, gate_in, own_sem.at[2])
@@ -247,7 +247,6 @@
             )
         signal_in[part, me] = signal[part, me] * scale
         signal_copies.append(copies)
-    scale_out[...] = scale
 
     chunks = fh.shape[0]
     chunk = fh.shape[2] // 2
@@ -268,10 +267,13 @@
         spectrum[index] = transform(halved_filter, index)
         return carry
 
-    def invert(block):
+    weights = column(skip[me], count, width)
+
+    def invert(part, block):
         both = jnp.dot(product[...], ih[block], preferred_element_type=jnp.float32)
         small = jnp.dot(product[:sub, :], il[block], preferred_element_type=jnp.float32)
-        return both[:sub] + (both[sub:] + small)
+        conv = both[:sub] + (both[sub:] + small)
+        return conv + weights[part * sub : (part + 1) * sub] * signal_in[part, block]
 
     own_filter.wait()
     for copy in filter_copies:
@@ -304,11 +306,11 @@
             tables[3].wait()
         for step in order:
             to = lax.rem(me + step, groups)
-            conv_out[part, to] = invert(to)
+            conv_out[part, to] = invert(part, to)
             conv_copies.append(
                 send(part * groups + step, step, conv_out.at[part, to], conv_in.at[me, part], c_send, c_recv)
             )
-        conv_out[part, me] = invert(me)
+        conv_out[part, me] = invert(part, me)
         conv_copies.append(local(conv_out.at[part, me], conv_in.at[me, part], own_sem.at[3 + part]))
     for copy in conv_copies:
         copy.wait()
@@ -328,11 +330,11 @@
     f32, bf16 = jnp.float32, jnp.bfloat16
     pair = pltpu.SemaphoreType.DMA((parts * groups,))
     ring = pltpu.SemaphoreType.DMA((peers,))
-    conv, scale = pl.pallas_call(
+    conv = pl.pallas_call(
         functools.partial(conv_kernel, groups, peers),
-        out_shape=[jax.ShapeDtypeStruct((groups, parts, sub, width), f32), jax.ShapeDtypeStruct((1, width), f32)],
-        in_specs=[hbm, hbm, hbm, vmem, hbm, hbm, hbm, hbm],
-        out_specs=[hbm, vmem],
+        out_shape=jax.ShapeDtypeStruct((groups, parts, sub, width), f32),
+        in_specs=[hbm, hbm, hbm, vmem, vmem, hbm, hbm, hbm, hbm],
+        out_specs=hbm,
         scratch_shapes=[
             pltpu.VMEM(tables[0].shape, bf16),
             pltpu.VMEM(tables[1].shape, bf16),
@@ -357,9 +359,11 @@
         compiler_params=pltpu.CompilerParams(
             collective_id=0, has_side_effects=True, vmem_limit_bytes=56 * 1024 * 1024
         ),
-    )(hidden, gate_in, filters, norm_gain.reshape(groups, 1, count), *tables)
-    signal = gate_in.astype(f32) * (hidden.astype(f32) * norm_gain[:, None]) * scale
-    mixed = gate_out.astype(f32) * (conv.reshape(channels, width) + skip_weight[:, None] * signal)
+    )(
+        hidden, gate_in, filters,
+        norm_gain.reshape(groups, 1, count), skip_weight.reshape(groups, 1, count), *tables,
+    )
+    mixed = gate_out.astype(f32) * conv.reshape(channels, width)
     return mixed.astype(bf16)
 
 

time: 32.5 us -> 31.6 us (0.972)
  Pallas kernels: 30.2 us -> 29.6 us
    pallas_call x1, Pallas kernels: 30.2 us -> 29.6 us  [fused(): pl.pallas_call(functools.partial(conv_kernel, groups, peers), out_shape=j...]
where the time goes in v4:
time: 31.6 us; the launch traced here: 31.4 us
  Pallas kernels  29.6 us (94%)
  other arithmetic  1.8 us (6%)
    pallas_call x1, Pallas kernels, fused(): pl.pallas_call(functools.partial(conv_kernel, groups, peers), out_shape=j...  29.6 us
    convert_element_type x1, other arithmetic, fused(): return mixed.astype(bf16)  1.8 us

profile of v4, /device:TPU:0, one launch (start us, length us, event | category | flops | bytes accessed | tf_op | source)
XLA Modules:
  0.0 31.4 jit_solution(11623895400952581221)
XLA Ops:
  0.0 0.0 copy-start
  0.0 29.6 %shard_map.100 = f32[4,2,64,256]{3,2,1,0:T(8,128)} custom-call(bf16[512,256]{1,0:T(8,128)(2,1)} %hidden_hbm.1, bf16[512,256]{1,0:T(8,128)(2,1)} %gate_hbm.1, f32[512,256]{1,0:T(8,128)} %filters.1, f32[4,1,128]{2,1,0:T(1,128)} %bitcast.6, f32[4,1,128]{2,1,0:T(1,128)} %bitcast.7, bf16[4,1024,512]{2,1,0:T(8,128)(2,1)} %constant.8.clone.fwd_hi, ...), custom_call_target="tpu_custom_call" | custom-call | tf_op jit(solution)/shard_map/pallas_call | solution.py:333
  29.6 0.0 copy-done
  29.6 1.8 %fusion = bf16[512,256]{1,0:T(8,128)(2,1)} fusion(f32[4,2,64,256]{3,2,1,0:T(8,128)} %shard_map.100, bf16[512,256]{1,0:T(8,128)(2,1)S(1)} %copy-done), kind=kLoop, calls=%fused_computation.1 | loop fusion | flops 393216 | bytes 1048576 | tf_op jit(solution)/shard_map/convert_element_type | solution.py:367
Async XLA Ops:
  0.0 29.6 %copy-start = (bf16[512,256]{1,0:T(8,128)(2,1)S(1)}, bf16[512,256]{1,0:T(8,128)(2,1)}, u32[]{:S(2)}) copy-start(bf16[512,256]{1,0:T(8,128)(2,1)} %param.12) | copy-start | bytes 786436

commit v5 on v4

--- a/solution.py
+++ b/solution.py
@@ -193,13 +193,6 @@
         local(source, target, table_sem.at[index])
         for index, (source, target) in enumerate(((fwd_hi, fh), (fwd_lo, fl), (inv_hi, ih), (inv_lo, il)))
     ]
-    own_hidden.wait()
-    partial = jnp.zeros((1, width), jnp.float32)
-    for block in range(groups):
-        activity = hidden[block * count : (block + 1) * count, :].astype(jnp.float32)
-        partial = partial + jnp.sum(activity * activity, axis=0, keepdims=True)
-    local_sum[...] = partial
-    sums[row] = partial
     pl.semaphore_wait(barrier, groups + peers - 2)
 
     order = [groups // 2] + [s for s in range(1, groups) if s != groups // 2]
@@ -215,6 +208,13 @@
         )
         for step in range(1, groups)
     ]
+    own_hidden.wait()
+    partial = jnp.zeros((1, width), jnp.float32)
+    for block in range(groups):
+        activity = hidden[block * count : (block + 1) * count, :].astype(jnp.float32)
+        partial = partial + jnp.sum(activity * activity, axis=0, keepdims=True)
+    local_sum[...] = partial
+    sums[row] = partial
     sum_copies = []
     for step in range(1, peers):
         copy = pltpu.make_async_remote_copy(

time: 31.6 us -> 31.6 us (level)
  no operation moved by 1% of the time
where the time goes in v5:
time: 31.6 us; the launch traced here: 31.4 us
  Pallas kernels  29.6 us (94%)
  other arithmetic  1.8 us (6%)
    pallas_call x1, Pallas kernels, fused(): pl.pallas_call(functools.partial(conv_kernel, groups, peers), out_shape=j...  29.6 us
    convert_element_type x1, other arithmetic, fused(): return mixed.astype(bf16)  1.8 us

profile of v5, /device:TPU:0, one launch (start us, length us, event | category | flops | bytes accessed | tf_op | source)
XLA Modules:
  0.0 31.4 jit_solution(12852328255859086775)
XLA Ops:
  0.0 0.0 copy-start
  0.0 29.6 %shard_map.100 = f32[4,2,64,256]{3,2,1,0:T(8,128)} custom-call(bf16[512,256]{1,0:T(8,128)(2,1)} %hidden_hbm.1, bf16[512,256]{1,0:T(8,128)(2,1)} %gate_hbm.1, f32[512,256]{1,0:T(8,128)} %filters.1, f32[4,1,128]{2,1,0:T(1,128)} %bitcast.6, f32[4,1,128]{2,1,0:T(1,128)} %bitcast.7, bf16[4,1024,512]{2,1,0:T(8,128)(2,1)} %constant.8.clone.fwd_hi, ...), custom_call_target="tpu_custom_call" | custom-call | tf_op jit(solution)/shard_map/pallas_call | solution.py:333
  29.6 0.0 copy-done
  29.6 1.8 %fusion = bf16[512,256]{1,0:T(8,128)(2,1)} fusion(f32[4,2,64,256]{3,2,1,0:T(8,128)} %shard_map.100, bf16[512,256]{1,0:T(8,128)(2,1)S(1)} %copy-done), kind=kLoop, calls=%fused_computation.1 | loop fusion | flops 393216 | bytes 1048576 | tf_op jit(solution)/shard_map/convert_element_type | solution.py:367
Async XLA Ops:
  0.0 29.6 %copy-start = (bf16[512,256]{1,0:T(8,128)(2,1)S(1)}, bf16[512,256]{1,0:T(8,128)(2,1)}, u32[]{:S(2)}) copy-start(bf16[512,256]{1,0:T(8,128)(2,1)} %param.12) | copy-start | bytes 786436
